TPU v7x, 256 devices: a whole 4x4x8 slice. The times are simulated.
256 devices in a mesh: fibre: 2 (over core), chan: 128 (over z, x, y).
Axes of the slice: x: 4, y: 4, z: 8, core: 2. Of those that a mesh axis runs over, the one named last changes fastest.
Arguments:
- raw: bfloat16 [32768, 4096], P(('fibre', 'chan'))
- starts: int32 [4], replicated, may hold values from 0 to 3072, as said below
- ref_ids: int32 [64], replicated, may hold values from 0 to 32767, as said below
- near_ids: int32 [32768, 8], P(('fibre', 'chan')), may hold values from 0 to 32767, as said below
- cross_ids: int32 [32768, 2], P(('fibre', 'chan')), may hold values from 0 to 255
- cross_mask: int32 [32768, 2], P(('fibre', 'chan')), may hold values 0 or 1
- export_loc: int32 [256], P(('fibre', 'chan')), may hold values from 0 to 127
Outputs:
- correlations: bfloat16 [32768, 64, 512], P(('fibre', 'chan'))
Inputs may be any that keep to these rules, and one draw needn't show every extreme that they name: starts[3] is 3072. `ref_ids`: distinct channel ids. `near_ids`: each neighbour lies on the same route as its channel (route = id // 16384) and at most 16 channels away from it.
All inputs are finite; a program needn't handle non-finite values. No bound on the sum of `cross_mask` on one device may be relied on, other than what follows from the above.
Results may differ from a plain program's by a relative error of at most 0.0063.
The roundings to bfloat16 on the way count: a program that leaves them out, or rounds other values in their place, can miss the bound.
Values may be sent and summed in bfloat16 or wider, within the bound.
A program may use at most 128 MiB of HBM per device.

v0:
```python
import math
import jax
import jax.numpy as jnp
from jax import lax
from jax.sharding import PartitionSpec as P

SEG = 1024
SEGS = 4
REFS = 64
LAGS = 512
NN = 8
HALO = 16


def with_halo(block, sides, width):
    for axis, dim in sides:
        count = lax.axis_size(axis)
        forward = [(i, i + 1) for i in range(count - 1)]
        backward = [(target, source) for source, target in forward]
        low = lax.ppermute(
            lax.slice_in_dim(block, block.shape[dim] - width, None, axis=dim), axis, forward
        )
        high = lax.ppermute(lax.slice_in_dim(block, 0, width, axis=dim), axis, backward)
        block = jnp.concatenate([low, block, high], axis=dim)
    return block


def forward_table():
    nbins = SEG // 2
    sample = jnp.arange(SEG, dtype=jnp.int32)
    freq = jnp.arange(nbins, dtype=jnp.int32)
    phase = jnp.mod(sample[:, None] * freq[None, :], SEG).astype(jnp.float32)
    theta = phase * (2.0 * math.pi / SEG)
    keep = (freq > 0).astype(jnp.float32)[None, :]
    return jnp.concatenate([jnp.cos(theta) * keep, -jnp.sin(theta)], 1).astype(jnp.bfloat16)


def lag_table():
    nbins = SEG // 2
    freq = jnp.arange(nbins, dtype=jnp.int32)
    lag = jnp.arange(LAGS, dtype=jnp.int32) - LAGS // 2
    phase = jnp.mod(freq[:, None] * lag[None, :], SEG).astype(jnp.float32)
    theta = phase * (2.0 * math.pi / SEG)
    scale = 1.0 / math.sqrt(nbins)
    table = jnp.concatenate([jnp.cos(theta) * scale, -jnp.sin(theta) * scale], 0)
    return table.astype(jnp.bfloat16)


def per_device(raw, starts, ref_ids, near_ids, cross_ids, cross_mask, export_loc):
    nbins = SEG // 2
    width = SEGS * SEG
    local_ch = raw.shape[0]
    block_base = lax.axis_index(("fibre", "chan")) * local_ch
    pieces = [lax.dynamic_slice_in_dim(raw, starts[s], SEG, 1) for s in range(SEGS)]
    segment = jnp.stack(pieces, 1)
    spectrum = jnp.dot(
        segment.reshape(local_ch * SEGS, SEG), forward_table(), preferred_element_type=jnp.float32
    )
    power = jnp.sum(spectrum * spectrum, -1, keepdims=True) / nbins
    whitened = (spectrum / jnp.sqrt(power + 1e-06)).astype(jnp.bfloat16)
    flat = whitened.reshape(local_ch, width)
    columns = jnp.arange(local_ch, dtype=jnp.int32)
    pick = (ref_ids[:, None] - block_base == columns[None, :]).astype(jnp.bfloat16)
    selected = jnp.dot(pick, flat, preferred_element_type=jnp.float32)
    references = lax.psum(selected, ("fibre", "chan")).astype(jnp.bfloat16)
    extended = with_halo(flat, (("chan", 0),), HALO)
    ext_rows = local_ch + 2 * HALO
    position = near_ids - (block_base - HALO)
    near_count = jnp.sum(
        (position[:, :, None] == jnp.arange(ext_rows, dtype=jnp.int32)[None, None, :]).astype(
            jnp.float32
        ),
        1,
    )
    total = flat.astype(jnp.float32) + jnp.dot(
        near_count.astype(jnp.bfloat16), extended, preferred_element_type=jnp.float32
    )
    exported = jnp.take(flat, export_loc, axis=0)
    live = cross_mask == 1
    piece = lax.all_gather(exported, ("fibre", "chan"), axis=0, tiled=True)
    slots = jnp.arange(piece.shape[0], dtype=jnp.int32)
    hits = (cross_ids[:, :, None] == slots[None, None, :]) & live[:, :, None]
    weights = jnp.sum(hits.astype(jnp.float32), 1).astype(jnp.bfloat16)
    crossing = jnp.dot(weights, piece, preferred_element_type=jnp.float32)
    count = 1.0 + NN + jnp.sum(cross_mask.astype(jnp.float32), 1)
    smoothed = ((total + crossing) / count[:, None]).astype(jnp.bfloat16)
    kernel = lag_table()
    ref_split = references.reshape(REFS, SEGS, SEG)
    ref_re = ref_split[..., :nbins]
    ref_im = ref_split[..., nbins:]
    group = math.gcd(local_ch, 32)

    def correlate(rows):
        a_re = rows[..., :nbins]
        a_im = rows[..., nbins:]
        g_re = jnp.einsum(
            "csf,rsf->crf", a_re, ref_re, preferred_element_type=jnp.float32
        ) + jnp.einsum("csf,rsf->crf", a_im, ref_im, preferred_element_type=jnp.float32)
        g_im = jnp.einsum(
            "csf,rsf->crf", a_im, ref_re, preferred_element_type=jnp.float32
        ) - jnp.einsum("csf,rsf->crf", a_re, ref_im, preferred_element_type=jnp.float32)
        cross = (jnp.concatenate([g_re, g_im], -1) / SEGS).astype(jnp.bfloat16)
        out = jnp.dot(cross.reshape(group * REFS, SEG), kernel, preferred_element_type=jnp.float32)
        return out.astype(jnp.bfloat16).reshape(group, REFS, LAGS)

    result = lax.map(correlate, smoothed.reshape(local_ch // group, group, SEGS, SEG))
    return result.reshape(local_ch, REFS, LAGS)


def solution(mesh):
    in_specs = (
        P(("fibre", "chan"), None),
        P(),
        P(),
        P(("fibre", "chan"), None),
        P(("fibre", "chan"), None),
        P(("fibre", "chan"), None),
        P(("fibre", "chan")),
    )
    out_specs = P(("fibre", "chan"), None, None)
    return jax.shard_map(
        per_device, mesh=mesh, in_specs=in_specs, out_specs=out_specs, check_vma=False
    )
```

profile of v0, /device:TPU:1, one launch (start us, length us, event | category | flops | bytes accessed | tf_op | source)
XLA Modules:
  0.0 315.5 jit_solution(655089644088672558)
XLA Ops:
  6.5 1.5 fusion.53
  13.1 8.0 %negate_convert_fusion = bf16[1024,512]{1,0:T(8,128)(2,1)S(1)} fusion(), kind=kLoop, calls=%fused_computation.36 | loop fusion | flops 8388608 | bytes 1048576 | tf_op jit(solution)/shard_map/convert.3
  23.6 1.9 dynamic-slice_bitcast_fusion.3
  26.7 7.9 %multiply_convert_fusion = bf16[1024,512]{1,0:T(8,128)(2,1)S(1)} fusion(f32[512]{0:T(512)S(1)} %fusion.48), kind=kLoop, calls=%fused_computation.37 | loop fusion | flops 8388608 | bytes 1050624 | tf_op jit(solution)/shard_map/convert.2
  34.7 1.3 multiply_reduce_fusion
  38.5 4.0 %collective-permute-start = (bf16[16,4096]{1,0:T(8,128)(2,1)S(1)}, bf16[16,4096]{1,0:T(8,128)(2,1)S(1)}, u32[]{:S(2)}, u32[]{:S(2)}) collective-permute-start(bf16[16,4096]{1,0:T(8,128)(2,1)S(1)} %slice.41), channel_id=1, source_target_pairs={{0,1},{1,2},{2,3},{3,4},{4,5},{5,6},{6,7},{7,8},{8,9},{9,10},{10,1... | collective-permute-start | bytes 393224 | tf_op jit(solution)/shard_map/ppermute | solution.py:20
  42.6 1.3 collective-permute-start.1
  44.3 88.9 %all-reduce.1 = bf16[64,4096]{1,0:T(8,128)(2,1)S(1)} all-reduce(f32[64,4096]{1,0:T(8,128)S(1)} %fusion.45), channel_id=1, replica_groups=mesh['fibre'=2,'chan'=128] {'fibre','chan'}, use_global_device_ids=true, to_apply=%region_4.5 | all-reduce | flops 262144 | bytes 1572864 | tf_op jit(solution)/shard_map/psum | solution.py:65
  133.8 1.1 copy.48
  134.9 1.1 copy.49
  136.3 4.5 %multiply_convert_fusion.2 = (bf16[512,512]{1,0:T(8,128)(2,1)S(1)}, bf16[512,512]{1,0:T(8,128)(2,1)S(1)}) fusion(s32[512]{0:T(512)S(1)} %iota_add_fusion), kind=kLoop, calls=%fused_computation.55 | loop fusion | flops 4980736 | bytes 1050624 | tf_op jit(solution)/shard_map/convert
  140.8 1.0 pad_maximum_fusion.1
  141.9 16.6 %all-gather.3.cloned.1.call-done = bf16[256,1,4096]{2,1,0:T(2,128)(2,1)} async-done(((bf16[1,1,4096]{2,1,0:T(2,128)(2,1)}), bf16[256,1,4096]{2,1,0:T(2,128)(2,1)}) %all-gather.3.cloned.1.call-update) | async-done | bytes 2097168 | tf_op jit(solution)/shard_map/all_gather | solution.py:80
  158.5 4.7 %fusion.25 = f32[128,4096]{1,0:T(8,128)S(1)} fusion(bf16[256,1,4096]{2,1,0:T(2,128)(2,1)} %all-gather.3.cloned.1.call-done, bf16[128,256]{1,0:T(8,128)(2,1)S(1)} %convert_reduce_fusion.1), kind=kOutput, calls=%fused_computation.31 | convolution fusion | flops 268435456 | bytes 4259840 | tf_op jit(solution)/shard_map/dot_general | solution.py:84
  164.9 143.8 %while.11 = (s32[]{:T(128)}, bf16[4,32,64,512]{3,2,1,0:T(8,128)(2,1)}, bf16[4,32,4,1024]{3,2,1,0:T(4,128)(2,1)S(1)}, bf16[64,4,512]{0,1,2:T(4,128)(2,1)S(1)}, bf...) while((s32[]{:T(128)}, ...), condition=%wide.region_6.7_spmd, body=%wide.region_5.6_spmd.sunk | while | flops 2190475264 | bytes 77595424 | solution.py:106
  166.8 1.3 fusion.87
  168.1 4.9 %add_bitcast_fusion.2 = f32[32,64,512]{1,0,2:T(8,128)} fusion(f32[512,32,64]{2,1,0:T(8,128)S(1)} %fusion.87, bf16[64,4,512]{0,1,2:T(4,128)(2,1)S(1)} %copy-done.6, bf16[1,32,4,1024]{1,2,3,0:T(4,128)(2,1)S(1)} %copy.57), kind=kOutput, calls=%fused_computation.3.clone.1 | convolution fusion | flops 9437184 | bytes 8912896 | tf_op jit(solution)/shard_map/while/body/eval_jaxpr/csf,rsf->crf/dot_general | solution.py:98
  173.1 6.9 %copy.59 = f32[32,64,512]{2,1,0:T(8,128)} copy(f32[32,64,512]{1,0,2:T(8,128)} %add_bitcast_fusion.2) | data formatting | bytes 8388608 | tf_op jit(solution)/shard_map/while/body/eval_jaxpr/add | solution.py:96
  180.0 1.3 fusion.86
  181.3 4.9 %subtract_bitcast_fusion.2 = f32[32,64,512]{1,0,2:T(8,128)} fusion(f32[512,32,64]{2,1,0:T(8,128)S(1)} %fusion.86, bf16[64,4,512]{0,1,2:T(4,128)(2,1)S(1)} %copy-done.7, bf16[1,32,4,1024]{1,2,3,0:T(4,128)(2,1)S(1)} %copy.57), kind=kOutput, calls=%fused_computation.2.clone.1 | convolution fusion | flops 9437184 | bytes 8912896 | tf_op jit(solution)/shard_map/while/body/eval_jaxpr/csf,rsf->crf/dot_general | solution.py:101
  186.2 6.9 %copy.58 = f32[32,64,512]{2,1,0:T(8,128)} copy(f32[32,64,512]{1,0,2:T(8,128)} %subtract_bitcast_fusion.2) | data formatting | bytes 8388608 | tf_op jit(solution)/shard_map/while/body/eval_jaxpr/sub | solution.py:99
  193.2 5.8 %fusion.88 = bf16[2048,512]{1,0:T(8,128)(2,1)S(1)} fusion(bf16[1024,512]{1,0:T(8,128)(2,1)S(1)} %copy-done.2, f32[2048,512]{1,0:T(8,128)} %bitcast.74, f32[2048,512]{1,0:T(8,128)} %bitcast.73), kind=kOutput, calls=%fused_computation.6.clone.1 | convolution fusion | flops 2154823680 | bytes 11534336 | tf_op jit(solution)/shard_map/while/body/eval_jaxpr/dot_general | solution.py:103
  199.0 1.6 constant_dynamic-update-slice_fusion.2
  200.8 1.0 copy-done
  202.7 1.3 fusion.87
  204.1 4.9 %add_bitcast_fusion.2 = f32[32,64,512]{1,0,2:T(8,128)} fusion(f32[512,32,64]{2,1,0:T(8,128)S(1)} %fusion.87, bf16[64,4,512]{0,1,2:T(4,128)(2,1)S(1)} %copy-done.6, bf16[1,32,4,1024]{1,2,3,0:T(4,128)(2,1)S(1)} %copy.57), kind=kOutput, calls=%fused_computation.3.clone.1 | convolution fusion | flops 9437184 | bytes 8912896 | tf_op jit(solution)/shard_map/while/body/eval_jaxpr/csf,rsf->crf/dot_general | solution.py:98
  209.0 6.9 %copy.59 = f32[32,64,512]{2,1,0:T(8,128)} copy(f32[32,64,512]{1,0,2:T(8,128)} %add_bitcast_fusion.2) | data formatting | bytes 8388608 | tf_op jit(solution)/shard_map/while/body/eval_jaxpr/add | solution.py:96
  215.9 1.3 fusion.86
  217.2 4.9 %subtract_bitcast_fusion.2 = f32[32,64,512]{1,0,2:T(8,128)} fusion(f32[512,32,64]{2,1,0:T(8,128)S(1)} %fusion.86, bf16[64,4,512]{0,1,2:T(4,128)(2,1)S(1)} %copy-done.7, bf16[1,32,4,1024]{1,2,3,0:T(4,128)(2,1)S(1)} %copy.57), kind=kOutput, calls=%fused_computation.2.clone.1 | convolution fusion | flops 9437184 | bytes 8912896 | tf_op jit(solution)/shard_map/while/body/eval_jaxpr/csf,rsf->crf/dot_general | solution.py:101
  222.2 6.9 %copy.58 = f32[32,64,512]{2,1,0:T(8,128)} copy(f32[32,64,512]{1,0,2:T(8,128)} %subtract_bitcast_fusion.2) | data formatting | bytes 8388608 | tf_op jit(solution)/shard_map/while/body/eval_jaxpr/sub | solution.py:99
  229.1 5.8 %fusion.88 = bf16[2048,512]{1,0:T(8,128)(2,1)S(1)} fusion(bf16[1024,512]{1,0:T(8,128)(2,1)S(1)} %copy-done.2, f32[2048,512]{1,0:T(8,128)} %bitcast.74, f32[2048,512]{1,0:T(8,128)} %bitcast.73), kind=kOutput, calls=%fused_computation.6.clone.1 | convolution fusion | flops 2154823680 | bytes 11534336 | tf_op jit(solution)/shard_map/while/body/eval_jaxpr/dot_general | solution.py:103
  235.0 1.6 constant_dynamic-update-slice_fusion.2
  238.7 1.3 fusion.87
  240.0 4.9 %add_bitcast_fusion.2 = f32[32,64,512]{1,0,2:T(8,128)} fusion(f32[512,32,64]{2,1,0:T(8,128)S(1)} %fusion.87, bf16[64,4,512]{0,1,2:T(4,128)(2,1)S(1)} %copy-done.6, bf16[1,32,4,1024]{1,2,3,0:T(4,128)(2,1)S(1)} %copy.57), kind=kOutput, calls=%fused_computation.3.clone.1 | convolution fusion | flops 9437184 | bytes 8912896 | tf_op jit(solution)/shard_map/while/body/eval_jaxpr/csf,rsf->crf/dot_general | solution.py:98
  245.0 6.9 %copy.59 = f32[32,64,512]{2,1,0:T(8,128)} copy(f32[32,64,512]{1,0,2:T(8,128)} %add_bitcast_fusion.2) | data formatting | bytes 8388608 | tf_op jit(solution)/shard_map/while/body/eval_jaxpr/add | solution.py:96
  251.9 1.3 fusion.86
  253.2 4.9 %subtract_bitcast_fusion.2 = f32[32,64,512]{1,0,2:T(8,128)} fusion(f32[512,32,64]{2,1,0:T(8,128)S(1)} %fusion.86, bf16[64,4,512]{0,1,2:T(4,128)(2,1)S(1)} %copy-done.7, bf16[1,32,4,1024]{1,2,3,0:T(4,128)(2,1)S(1)} %copy.57), kind=kOutput, calls=%fused_computation.2.clone.1 | convolution fusion | flops 9437184 | bytes 8912896 | tf_op jit(solution)/shard_map/while/body/eval_jaxpr/csf,rsf->crf/dot_general | solution.py:101
  258.1 6.9 %copy.58 = f32[32,64,512]{2,1,0:T(8,128)} copy(f32[32,64,512]{1,0,2:T(8,128)} %subtract_bitcast_fusion.2) | data formatting | bytes 8388608 | tf_op jit(solution)/shard_map/while/body/eval_jaxpr/sub | solution.py:99
  265.1 5.8 %fusion.88 = bf16[2048,512]{1,0:T(8,128)(2,1)S(1)} fusion(bf16[1024,512]{1,0:T(8,128)(2,1)S(1)} %copy-done.2, f32[2048,512]{1,0:T(8,128)} %bitcast.74, f32[2048,512]{1,0:T(8,128)} %bitcast.73), kind=kOutput, calls=%fused_computation.6.clone.1 | convolution fusion | flops 2154823680 | bytes 11534336 | tf_op jit(solution)/shard_map/while/body/eval_jaxpr/dot_general | solution.py:103
  270.9 1.6 constant_dynamic-update-slice_fusion.2
  274.6 1.3 fusion.87
  276.0 4.9 %add_bitcast_fusion.2 = f32[32,64,512]{1,0,2:T(8,128)} fusion(f32[512,32,64]{2,1,0:T(8,128)S(1)} %fusion.87, bf16[64,4,512]{0,1,2:T(4,128)(2,1)S(1)} %copy-done.6, bf16[1,32,4,1024]{1,2,3,0:T(4,128)(2,1)S(1)} %copy.57), kind=kOutput, calls=%fused_computation.3.clone.1 | convolution fusion | flops 9437184 | bytes 8912896 | tf_op jit(solution)/shard_map/while/body/eval_jaxpr/csf,rsf->crf/dot_general | solution.py:98
  280.9 6.9 %copy.59 = f32[32,64,512]{2,1,0:T(8,128)} copy(f32[32,64,512]{1,0,2:T(8,128)} %add_bitcast_fusion.2) | data formatting | bytes 8388608 | tf_op jit(solution)/shard_map/while/body/eval_jaxpr/add | solution.py:96
  287.8 1.3 fusion.86
  289.1 4.9 %subtract_bitcast_fusion.2 = f32[32,64,512]{1,0,2:T(8,128)} fusion(f32[512,32,64]{2,1,0:T(8,128)S(1)} %fusion.86, bf16[64,4,512]{0,1,2:T(4,128)(2,1)S(1)} %copy-done.7, bf16[1,32,4,1024]{1,2,3,0:T(4,128)(2,1)S(1)} %copy.57), kind=kOutput, calls=%fused_computation.2.clone.1 | convolution fusion | flops 9437184 | bytes 8912896 | tf_op jit(solution)/shard_map/while/body/eval_jaxpr/csf,rsf->crf/dot_general | solution.py:101
  294.1 6.9 %copy.58 = f32[32,64,512]{2,1,0:T(8,128)} copy(f32[32,64,512]{1,0,2:T(8,128)} %subtract_bitcast_fusion.2) | data formatting | bytes 8388608 | tf_op jit(solution)/shard_map/while/body/eval_jaxpr/sub | solution.py:99
  301.0 5.8 %fusion.88 = bf16[2048,512]{1,0:T(8,128)(2,1)S(1)} fusion(bf16[1024,512]{1,0:T(8,128)(2,1)S(1)} %copy-done.2, f32[2048,512]{1,0:T(8,128)} %bitcast.74, f32[2048,512]{1,0:T(8,128)} %bitcast.73), kind=kOutput, calls=%fused_computation.6.clone.1 | convolution fusion | flops 2154823680 | bytes 11534336 | tf_op jit(solution)/shard_map/while/body/eval_jaxpr/dot_general | solution.py:103
  306.8 1.6 constant_dynamic-update-slice_fusion.2
  (102 shorter events, 13.6 us)
Async XLA Ops:
  6.5 151.9 %all-gather.3.cloned.1.call-start = ((), (), s32[]{:S(2)}) async-start(), calls=%async_computation | async-start | bytes 4210688 | tf_op jit(solution)/shard_map/all_gather | solution.py:80
  36.3 7.6 %copy-start.11 = (s32[64]{0:T(128)S(1)}, s32[64]{0:T(128)}, u32[]{:S(2)}) copy-start(s32[64]{0:T(128)} %param.11) | copy-start | bytes 772
  38.5 124.7 %collective-permute-start = (bf16[16,4096]{1,0:T(8,128)(2,1)S(1)}, bf16[16,4096]{1,0:T(8,128)(2,1)S(1)}, u32[]{:S(2)}, u32[]{:S(2)}) collective-permute-start(bf16[16,4096]{1,0:T(8,128)(2,1)S(1)} %slice.41), channel_id=1, source_target_pairs={{0,1},{1,2},{2,3},{3,4},{4,5},{5,6},{6,7},{7,8},{8,9},{9,10},{10,1... | collective-permute-start | bytes 393224 | tf_op jit(solution)/shard_map/ppermute | solution.py:20
  42.6 120.6 %collective-permute-start.1 = (bf16[16,4096]{1,0:T(8,128)(2,1)S(1)}, bf16[16,4096]{1,0:T(8,128)(2,1)S(1)}, u32[]{:S(2)}, u32[]{:S(2)}) collective-permute-start(bf16[16,4096]{1,0:T(8,128)(2,1)S(1)} %slice.43), channel_id=1, source_target_pairs={{1,0},{2,1},{3,2},{4,3},{5,4},{6,5},{7,6},{8,7},{9,8},{10,9},{11,1... | collective-permute-start | bytes 393224 | tf_op jit(solution)/shard_map/ppermute | solution.py:23
  133.2 2.9 copy-start.10
  133.2 2.9 copy-start.9
  133.2 3.0 copy-start.8
  163.8 1.0 copy-start.3
  164.9 1.0 copy-start
  166.8 1.3 copy-start.6
  173.1 6.9 %copy-start.4 = (bf16[64,4,512]{0,1,2:T(4,128)(2,1)S(1)}, bf16[64,4,512]{0,1,2:T(4,128)(2,1)}, u32[]{:S(2)}) copy-start(bf16[64,4,512]{0,1,2:T(4,128)(2,1)} %get-tuple-element.174) | copy-start | bytes 786436 | tf_op jit(solution)/shard_map/while
  180.0 1.3 copy-start.7
  186.2 6.9 %copy-start.2 = (bf16[1024,512]{1,0:T(8,128)(2,1)S(1)}, bf16[1024,512]{1,0:T(8,128)(2,1)}, u32[]{:S(2)}) copy-start(bf16[1024,512]{1,0:T(8,128)(2,1)} %get-tuple-element.163) | copy-start | bytes 3145732 | tf_op jit(solution)/shard_map/while
  199.0 1.6 copy-start.1
  199.0 1.8 copy-start.5
  200.8 1.0 copy-start
  202.7 1.3 copy-start.6
  209.0 6.9 %copy-start.4 = (bf16[64,4,512]{0,1,2:T(4,128)(2,1)S(1)}, bf16[64,4,512]{0,1,2:T(4,128)(2,1)}, u32[]{:S(2)}) copy-start(bf16[64,4,512]{0,1,2:T(4,128)(2,1)} %get-tuple-element.174) | copy-start | bytes 786436 | tf_op jit(solution)/shard_map/while
  215.9 1.3 copy-start.7
  222.2 6.9 %copy-start.2 = (bf16[1024,512]{1,0:T(8,128)(2,1)S(1)}, bf16[1024,512]{1,0:T(8,128)(2,1)}, u32[]{:S(2)}) copy-start(bf16[1024,512]{1,0:T(8,128)(2,1)} %get-tuple-element.163) | copy-start | bytes 3145732 | tf_op jit(solution)/shard_map/while
  234.9 1.6 copy-start.1
  234.9 1.8 copy-start.5
  236.8 1.0 copy-start
  238.7 1.3 copy-start.6
  245.0 6.9 %copy-start.4 = (bf16[64,4,512]{0,1,2:T(4,128)(2,1)S(1)}, bf16[64,4,512]{0,1,2:T(4,128)(2,1)}, u32[]{:S(2)}) copy-start(bf16[64,4,512]{0,1,2:T(4,128)(2,1)} %get-tuple-element.174) | copy-start | bytes 786436 | tf_op jit(solution)/shard_map/while
  251.9 1.3 copy-start.7
  258.1 6.9 %copy-start.2 = (bf16[1024,512]{1,0:T(8,128)(2,1)S(1)}, bf16[1024,512]{1,0:T(8,128)(2,1)}, u32[]{:S(2)}) copy-start(bf16[1024,512]{1,0:T(8,128)(2,1)} %get-tuple-element.163) | copy-start | bytes 3145732 | tf_op jit(solution)/shard_map/while
  270.9 1.6 copy-start.1
  270.9 1.8 copy-start.5
  272.7 1.0 copy-start
  274.6 1.3 copy-start.6
  280.9 6.9 %copy-start.4 = (bf16[64,4,512]{0,1,2:T(4,128)(2,1)S(1)}, bf16[64,4,512]{0,1,2:T(4,128)(2,1)}, u32[]{:S(2)}) copy-start(bf16[64,4,512]{0,1,2:T(4,128)(2,1)} %get-tuple-element.174) | copy-start | bytes 786436 | tf_op jit(solution)/shard_map/while
  287.8 1.3 copy-start.7
  294.1 6.9 %copy-start.2 = (bf16[1024,512]{1,0:T(8,128)(2,1)S(1)}, bf16[1024,512]{1,0:T(8,128)(2,1)}, u32[]{:S(2)}) copy-start(bf16[1024,512]{1,0:T(8,128)(2,1)} %get-tuple-element.163) | copy-start | bytes 3145732 | tf_op jit(solution)/shard_map/while
  306.8 1.6 copy-start.1
  306.8 1.8 copy-start.5
Sparse Core Ops, SparseCore 0:
  38.4 119.9 all-gather.2
where the time goes:
time: 316 us
  blocking collectives  88.9 us (28%)
  matrix products  80.2 us (25%)
  local copies, waits for them, and re-layouts  79.5 us (25%)
  other arithmetic  22.8 us (7%)
  between operations  21.9 us (7%)
  waiting for transfers between devices  16.6 us (5%)
  starting transfers between devices  5.32 us (2%)
    psum x1, blocking collectives, per_device(): references = lax.psum(selected, ('fibre', 'chan')).astype(jnp.bfloat16)  88.9 us
    add x4, local copies, waits for them, and re-layouts, correlate(): jnp.einsum('csf,rsf->crf', a_re, ref_re, preferred_element_type=jnp.float32)  27.7 us
    sub x4, local copies, waits for them, and re-layouts, correlate(): jnp.einsum('csf,rsf->crf', a_im, ref_re, preferred_element_type=jnp.float32)  27.7 us
    dot_general x4, matrix products, correlate(): jnp.dot(cross.reshape(group * REFS, SEG), kernel, preferred_element_type=...  23.2 us
    another operation x3, other arithmetic  20.4 us
    dot_general x4, matrix products, correlate(): jnp.einsum('csf,rsf->crf', a_re, ref_im, preferred_element_type=jnp.float32)  19.8 us
    dot_general x4, matrix products, correlate(): jnp.einsum('csf,rsf->crf', a_im, ref_im, preferred_element_type=jnp.float32)  19.8 us
    all_gather x1, waiting for transfers between devices, per_device(): piece = lax.all_gather(exported, ('fibre', 'chan'), axis=0, tiled=True)  16.6 us
  transfers between devices with their start and end apart: 3, of which 1 were waited for; matrix products, arithmetic and copies ran while one was open for 4% of the time, Pallas kernels for 0%

commit v1 on v0

--- a/solution.py
+++ b/solution.py
@@ -77,7 +77,12 @@
     )
     exported = jnp.take(flat, export_loc, axis=0)
     live = cross_mask == 1
-    piece = lax.all_gather(exported, ("fibre", "chan"), axis=0, tiled=True)
+    piece = jnp.concatenate(
+        lax.all_to_all(
+            jnp.stack([exported] * lax.axis_size(("fibre", "chan"))), ("fibre", "chan"), 0, 0
+        ),
+        axis=0,
+    )
     slots = jnp.arange(piece.shape[0], dtype=jnp.int32)
     hits = (cross_ids[:, :, None] == slots[None, None, :]) & live[:, :, None]
     weights = jnp.sum(hits.astype(jnp.float32), 1).astype(jnp.bfloat16)

time: 316 us -> 337 us (1.066)
  local copies, waits for them, and re-layouts: 79.5 us -> 96.7 us
  waiting for transfers between devices: 16.6 us -> 0.01 us
  starting transfers between devices: 5.32 us -> 21 us
  between operations: 21.9 us -> 8.48 us
  other arithmetic: 22.8 us -> 35.7 us
    all_gather x1 -> x0, waiting for transfers between devices: 16.6 us -> none  [per_device(): piece = lax.all_gather(exported, ('fibre', 'chan'), axis=0, tiled=True)]
    all_to_all x0 -> x1, starting transfers between devices: none -> 15.6 us  [per_device(): lax.all_to_all(jnp.stack([exported] * lax.axis_size(('fibre', 'chan'))),...]
    another operation x3 -> x4, other arithmetic: 20.4 us -> 33.9 us
    unnamed x12 -> x18, local copies, waits for them, and re-layouts: 2.5 us -> 12 us
    another operation x0 -> x2, local copies, waits for them, and re-layouts: none -> 6.78 us  [per_device(): jnp.stack([exported] * lax.axis_size(('fibre', 'chan')))]
  transfers between devices with their start and end apart: 3 -> 3, of which waited for: 1 -> 0; matrix products, arithmetic and copies ran while one was open for 4% -> 7% of each run, Pallas kernels for 0% -> 0%
where the time goes in v1:
time: 337 us; the launch traced here: 336 us
  local copies, waits for them, and re-layouts  96.7 us (29%)
  blocking collectives  91 us (27%)
  matrix products  82.5 us (24%)
  other arithmetic  35.7 us (11%)
  starting transfers between devices  21 us (6%)
  between operations  8.48 us (3%)
    psum x1, blocking collectives, per_device(): references = lax.psum(selected, ('fibre', 'chan')).astype(jnp.bfloat16)  91 us
    sub x4, local copies, waits for them, and re-layouts, correlate(): jnp.einsum('csf,rsf->crf', a_im, ref_re, preferred_element_type=jnp.float32)  27.7 us
    add x4, local copies, waits for them, and re-layouts, correlate(): jnp.einsum('csf,rsf->crf', a_re, ref_re, preferred_element_type=jnp.float32)  27.5 us
    dot_general x4, matrix products, correlate(): jnp.dot(cross.reshape(group * REFS, SEG), kernel, preferred_element_type=...  23.2 us
    another operation x3, other arithmetic  20.4 us
    dot_general x4, matrix products, correlate(): jnp.einsum('csf,rsf->crf', a_im, ref_im, preferred_element_type=jnp.float32)  19.7 us
    dot_general x4, matrix products, correlate(): jnp.einsum('csf,rsf->crf', a_re, ref_im, preferred_element_type=jnp.float32)  19.7 us
    all_to_all x1, starting transfers between devices, per_device(): lax.all_to_all(jnp.stack([exported] * lax.axis_size(('fibre', 'chan'))),...  15.6 us
  transfers between devices with their start and end apart: 3, of which 0 were waited for; matrix products, arithmetic and copies ran while one was open for 7% of the time, Pallas kernels for 0%

profile of v1, /device:TPU:1, one launch (start us, length us, event | category | flops | bytes accessed | tf_op | source)
XLA Modules:
  0.0 335.7 jit_solution(6123629360542432113)
XLA Ops:
  0.0 1.5 fusion.53
  6.5 8.0 %negate_convert_fusion = bf16[1024,512]{1,0:T(8,128)(2,1)S(1)} fusion(), kind=kLoop, calls=%fused_computation.36 | loop fusion | flops 8388608 | bytes 1048576 | tf_op jit(solution)/shard_map/convert.3
  17.0 1.9 dynamic-slice_bitcast_fusion.3
  20.2 7.9 %multiply_convert_fusion = bf16[1024,512]{1,0:T(8,128)(2,1)S(1)} fusion(f32[512]{0:T(512)S(1)} %fusion.48), kind=kLoop, calls=%fused_computation.37 | loop fusion | flops 8388608 | bytes 1050624 | tf_op jit(solution)/shard_map/convert.2
  28.1 1.3 multiply_reduce_fusion
  31.2 6.3 %stack.17 = bf16[256,1,4096]{2,1,0:T(2,128)(2,1)} broadcast(bf16[4096]{0:T(1024)(128)(2,1)S(1)} %fusion.46), dimensions={2} | broadcast | bytes 2105344 | tf_op jit(solution)/shard_map/stack | solution.py:82
  38.0 13.5 %reduce.2 = bf16[256,4096]{1,0:T(8,128)(2,1)S(1)} reduce(bf16[256,1,4096]{2,1,0:T(2,128)(2,1)} %stack.17, bf16[]{:T(256)} %broadcast.109), dimensions={1}, to_apply=%stack.17.reduce_sub_computation | reduce | bytes 4194306 | tf_op jit(solution)/shard_map/stack | solution.py:82
  51.5 2.8 reshape.97
  54.2 15.6 %all-to-all-start = ((bf16[256,2,2048]{2,1,0:T(2,128)(2,1)}), bf16[256,2,2048]{2,1,0:T(2,128)(2,1)S(1)}, u32[]{:S(2)}, u32[]{:S(2)}) async-start(bf16[256,2,2048]{2,1,0:T(2,128)(2,1)} %reshape.97), calls=%async_computation | async-start | bytes 4194304 | tf_op jit(solution)/shard_map/all_to_all | solution.py:81
  70.0 3.9 %collective-permute-start = (bf16[16,4096]{1,0:T(8,128)(2,1)S(1)}, bf16[16,4096]{1,0:T(8,128)(2,1)}, u32[]{:S(2)}, u32[]{:S(2)}) collective-permute-start(bf16[16,4096]{1,0:T(8,128)(2,1)S(1)} %slice.41), channel_id=1, source_target_pairs={{0,1},{1,2},{2,3},{3,4},{4,5},{5,6},{6,7},{7,8},{8,9},{9,10},{10,1... | collective-permute-start | bytes 393224 | tf_op jit(solution)/shard_map/ppermute | solution.py:20
  74.0 1.5 collective-permute-start.1
  75.5 1.6 fusion.45
  77.1 91.0 %all-reduce.1 = bf16[64,4096]{1,0:T(8,128)(2,1)} all-reduce(f32[64,4096]{1,0:T(8,128)S(1)} %fusion.45), channel_id=1, replica_groups=mesh['fibre'=2,'chan'=128] {'fibre','chan'}, use_global_device_ids=true, to_apply=%region_4.5 | all-reduce | flops 262144 | bytes 1572864 | tf_op jit(solution)/shard_map/psum | solution.py:65
  168.1 1.5 reshape.68
  172.3 4.5 %multiply_convert_fusion.2 = (bf16[512,512]{1,0:T(8,128)(2,1)S(1)}, bf16[512,512]{1,0:T(8,128)(2,1)S(1)}) fusion(s32[512]{0:T(512)S(1)} %iota_add_fusion), kind=kLoop, calls=%fused_computation.55 | loop fusion | flops 4980736 | bytes 1050624 | tf_op jit(solution)/shard_map/convert
  177.8 6.7 %reshape.98 = bf16[256,1,4096]{2,1,0:T(2,128)(2,1)} reshape(bf16[256,2,2048]{2,1,0:T(2,128)(2,1)S(1)} %all-to-all-done) | data formatting | bytes 4194304
  184.6 4.8 %fusion.25 = f32[128,4096]{1,0:T(8,128)S(1)} fusion(bf16[256,1,4096]{2,1,0:T(2,128)(2,1)} %reshape.98, bf16[128,256]{1,0:T(8,128)(2,1)S(1)} %convert_reduce_fusion.1), kind=kOutput, calls=%fused_computation.31 | convolution fusion | flops 268435456 | bytes 4259840 | tf_op jit(solution)/shard_map/dot_general | solution.py:89
  189.4 1.6 fusion.17
  192.1 143.6 %while.11 = (s32[]{:T(128)}, bf16[4,32,64,512]{3,2,1,0:T(8,128)(2,1)}, bf16[4,32,4,1024]{3,2,1,0:T(4,128)(2,1)S(1)}, bf16[64,4,512]{0,1,2:T(4,128)(2,1)S(1)}, bf...) while((s32[]{:T(128)}, ...), condition=%wide.region_6.7_spmd, body=%wide.region_5.6_spmd.sunk | while | flops 2190475264 | bytes 77595424 | solution.py:111
  194.0 1.3 fusion.87
  195.3 4.9 %add_bitcast_fusion.2 = f32[32,64,512]{1,0,2:T(8,128)} fusion(f32[512,32,64]{2,1,0:T(8,128)S(1)} %fusion.87, bf16[64,4,512]{0,1,2:T(4,128)(2,1)S(1)} %copy-done.8, bf16[1,32,4,1024]{1,2,3,0:T(4,128)(2,1)S(1)} %copy.57), kind=kOutput, calls=%fused_computation.3.clone.1 | convolution fusion | flops 9437184 | bytes 8912896 | tf_op jit(solution)/shard_map/while/body/eval_jaxpr/csf,rsf->crf/dot_general | solution.py:103
  200.2 6.9 %copy.59 = f32[32,64,512]{2,1,0:T(8,128)} copy(f32[32,64,512]{1,0,2:T(8,128)} %add_bitcast_fusion.2) | data formatting | bytes 8388608 | tf_op jit(solution)/shard_map/while/body/eval_jaxpr/add | solution.py:101
  208.4 4.9 %subtract_bitcast_fusion.2 = f32[32,64,512]{1,0,2:T(8,128)} fusion(f32[512,32,64]{2,1,0:T(8,128)S(1)} %fusion.86, bf16[64,4,512]{0,1,2:T(4,128)(2,1)S(1)} %copy-done.9, bf16[1,32,4,1024]{1,2,3,0:T(4,128)(2,1)S(1)} %copy.57), kind=kOutput, calls=%fused_computation.2.clone.1 | convolution fusion | flops 9437184 | bytes 8912896 | tf_op jit(solution)/shard_map/while/body/eval_jaxpr/csf,rsf->crf/dot_general | solution.py:106
  213.4 6.9 %copy.58 = f32[32,64,512]{2,1,0:T(8,128)} copy(f32[32,64,512]{1,0,2:T(8,128)} %subtract_bitcast_fusion.2) | data formatting | bytes 8388608 | tf_op jit(solution)/shard_map/while/body/eval_jaxpr/sub | solution.py:104
  220.3 5.8 %fusion.88 = bf16[2048,512]{1,0:T(8,128)(2,1)S(1)} fusion(bf16[1024,512]{1,0:T(8,128)(2,1)S(1)} %copy-done.4, f32[2048,512]{1,0:T(8,128)} %bitcast.72, f32[2048,512]{1,0:T(8,128)} %bitcast.71), kind=kOutput, calls=%fused_computation.6.clone.1 | convolution fusion | flops 2154823680 | bytes 11534336 | tf_op jit(solution)/shard_map/while/body/eval_jaxpr/dot_general | solution.py:108
  226.1 1.6 constant_dynamic-update-slice_fusion.2
  229.9 1.3 fusion.87
  231.2 4.9 %add_bitcast_fusion.2 = f32[32,64,512]{1,0,2:T(8,128)} fusion(f32[512,32,64]{2,1,0:T(8,128)S(1)} %fusion.87, bf16[64,4,512]{0,1,2:T(4,128)(2,1)S(1)} %copy-done.8, bf16[1,32,4,1024]{1,2,3,0:T(4,128)(2,1)S(1)} %copy.57), kind=kOutput, calls=%fused_computation.3.clone.1 | convolution fusion | flops 9437184 | bytes 8912896 | tf_op jit(solution)/shard_map/while/body/eval_jaxpr/csf,rsf->crf/dot_general | solution.py:103
  236.1 6.9 %copy.59 = f32[32,64,512]{2,1,0:T(8,128)} copy(f32[32,64,512]{1,0,2:T(8,128)} %add_bitcast_fusion.2) | data formatting | bytes 8388608 | tf_op jit(solution)/shard_map/while/body/eval_jaxpr/add | solution.py:101
  243.0 1.3 fusion.86
  244.3 4.9 %subtract_bitcast_fusion.2 = f32[32,64,512]{1,0,2:T(8,128)} fusion(f32[512,32,64]{2,1,0:T(8,128)S(1)} %fusion.86, bf16[64,4,512]{0,1,2:T(4,128)(2,1)S(1)} %copy-done.9, bf16[1,32,4,1024]{1,2,3,0:T(4,128)(2,1)S(1)} %copy.57), kind=kOutput, calls=%fused_computation.2.clone.1 | convolution fusion | flops 9437184 | bytes 8912896 | tf_op jit(solution)/shard_map/while/body/eval_jaxpr/csf,rsf->crf/dot_general | solution.py:106
  249.3 6.9 %copy.58 = f32[32,64,512]{2,1,0:T(8,128)} copy(f32[32,64,512]{1,0,2:T(8,128)} %subtract_bitcast_fusion.2) | data formatting | bytes 8388608 | tf_op jit(solution)/shard_map/while/body/eval_jaxpr/sub | solution.py:104
  256.2 5.8 %fusion.88 = bf16[2048,512]{1,0:T(8,128)(2,1)S(1)} fusion(bf16[1024,512]{1,0:T(8,128)(2,1)S(1)} %copy-done.4, f32[2048,512]{1,0:T(8,128)} %bitcast.72, f32[2048,512]{1,0:T(8,128)} %bitcast.71), kind=kOutput, calls=%fused_computation.6.clone.1 | convolution fusion | flops 2154823680 | bytes 11534336 | tf_op jit(solution)/shard_map/while/body/eval_jaxpr/dot_general | solution.py:108
  262.0 1.6 constant_dynamic-update-slice_fusion.2
  265.8 1.3 fusion.87
  267.1 4.9 %add_bitcast_fusion.2 = f32[32,64,512]{1,0,2:T(8,128)} fusion(f32[512,32,64]{2,1,0:T(8,128)S(1)} %fusion.87, bf16[64,4,512]{0,1,2:T(4,128)(2,1)S(1)} %copy-done.8, bf16[1,32,4,1024]{1,2,3,0:T(4,128)(2,1)S(1)} %copy.57), kind=kOutput, calls=%fused_computation.3.clone.1 | convolution fusion | flops 9437184 | bytes 8912896 | tf_op jit(solution)/shard_map/while/body/eval_jaxpr/csf,rsf->crf/dot_general | solution.py:103
  272.0 6.9 %copy.59 = f32[32,64,512]{2,1,0:T(8,128)} copy(f32[32,64,512]{1,0,2:T(8,128)} %add_bitcast_fusion.2) | data formatting | bytes 8388608 | tf_op jit(solution)/shard_map/while/body/eval_jaxpr/add | solution.py:101
  280.2 4.9 %subtract_bitcast_fusion.2 = f32[32,64,512]{1,0,2:T(8,128)} fusion(f32[512,32,64]{2,1,0:T(8,128)S(1)} %fusion.86, bf16[64,4,512]{0,1,2:T(4,128)(2,1)S(1)} %copy-done.9, bf16[1,32,4,1024]{1,2,3,0:T(4,128)(2,1)S(1)} %copy.57), kind=kOutput, calls=%fused_computation.2.clone.1 | convolution fusion | flops 9437184 | bytes 8912896 | tf_op jit(solution)/shard_map/while/body/eval_jaxpr/csf,rsf->crf/dot_general | solution.py:106
  285.2 6.9 %copy.58 = f32[32,64,512]{2,1,0:T(8,128)} copy(f32[32,64,512]{1,0,2:T(8,128)} %subtract_bitcast_fusion.2) | data formatting | bytes 8388608 | tf_op jit(solution)/shard_map/while/body/eval_jaxpr/sub | solution.py:104
  292.1 5.8 %fusion.88 = bf16[2048,512]{1,0:T(8,128)(2,1)S(1)} fusion(bf16[1024,512]{1,0:T(8,128)(2,1)S(1)} %copy-done.4, f32[2048,512]{1,0:T(8,128)} %bitcast.72, f32[2048,512]{1,0:T(8,128)} %bitcast.71), kind=kOutput, calls=%fused_computation.6.clone.1 | convolution fusion | flops 2154823680 | bytes 11534336 | tf_op jit(solution)/shard_map/while/body/eval_jaxpr/dot_general | solution.py:108
  297.9 1.6 constant_dynamic-update-slice_fusion.2
  301.7 1.3 fusion.87
  303.0 4.9 %add_bitcast_fusion.2 = f32[32,64,512]{1,0,2:T(8,128)} fusion(f32[512,32,64]{2,1,0:T(8,128)S(1)} %fusion.87, bf16[64,4,512]{0,1,2:T(4,128)(2,1)S(1)} %copy-done.8, bf16[1,32,4,1024]{1,2,3,0:T(4,128)(2,1)S(1)} %copy.57), kind=kOutput, calls=%fused_computation.3.clone.1 | convolution fusion | flops 9437184 | bytes 8912896 | tf_op jit(solution)/shard_map/while/body/eval_jaxpr/csf,rsf->crf/dot_general | solution.py:103
  307.9 6.9 %copy.59 = f32[32,64,512]{2,1,0:T(8,128)} copy(f32[32,64,512]{1,0,2:T(8,128)} %add_bitcast_fusion.2) | data formatting | bytes 8388608 | tf_op jit(solution)/shard_map/while/body/eval_jaxpr/add | solution.py:101
  316.1 4.9 %subtract_bitcast_fusion.2 = f32[32,64,512]{1,0,2:T(8,128)} fusion(f32[512,32,64]{2,1,0:T(8,128)S(1)} %fusion.86, bf16[64,4,512]{0,1,2:T(4,128)(2,1)S(1)} %copy-done.9, bf16[1,32,4,1024]{1,2,3,0:T(4,128)(2,1)S(1)} %copy.57), kind=kOutput, calls=%fused_computation.2.clone.1 | convolution fusion | flops 9437184 | bytes 8912896 | tf_op jit(solution)/shard_map/while/body/eval_jaxpr/csf,rsf->crf/dot_general | solution.py:106
  321.1 6.9 %copy.58 = f32[32,64,512]{2,1,0:T(8,128)} copy(f32[32,64,512]{1,0,2:T(8,128)} %subtract_bitcast_fusion.2) | data formatting | bytes 8388608 | tf_op jit(solution)/shard_map/while/body/eval_jaxpr/sub | solution.py:104
  328.0 5.8 %fusion.88 = bf16[2048,512]{1,0:T(8,128)(2,1)S(1)} fusion(bf16[1024,512]{1,0:T(8,128)(2,1)S(1)} %copy-done.4, f32[2048,512]{1,0:T(8,128)} %bitcast.72, f32[2048,512]{1,0:T(8,128)} %bitcast.71), kind=kOutput, calls=%fused_computation.6.clone.1 | convolution fusion | flops 2154823680 | bytes 11534336 | tf_op jit(solution)/shard_map/while/body/eval_jaxpr/dot_general | solution.py:108
  333.8 1.6 constant_dynamic-update-slice_fusion.2
  (110 shorter events, 20.4 us)
Async XLA Ops:
  30.4 7.0 %copy-start.2 = (bf16[128,4096]{1,0:T(8,128)(2,1)}, bf16[128,4096]{1,0:T(8,128)(2,1)S(1)}, u32[]{:S(2)}) copy-start(bf16[128,4096]{1,0:T(8,128)(2,1)S(1)} %reshape.65) | copy-start | bytes 3145732
  54.2 21.3 %copy-start.13 = (s32[64]{0:T(128)S(1)}, s32[64]{0:T(128)}, u32[]{:S(2)}) copy-start(s32[64]{0:T(128)} %param.11) | copy-start | bytes 772
  54.2 123.6 %all-to-all-start = ((bf16[256,2,2048]{2,1,0:T(2,128)(2,1)}), bf16[256,2,2048]{2,1,0:T(2,128)(2,1)S(1)}, u32[]{:S(2)}, u32[]{:S(2)}) async-start(bf16[256,2,2048]{2,1,0:T(2,128)(2,1)} %reshape.97), calls=%async_computation | async-start | bytes 4194304 | tf_op jit(solution)/shard_map/all_to_all | solution.py:81
  70.0 119.4 %collective-permute-start = (bf16[16,4096]{1,0:T(8,128)(2,1)S(1)}, bf16[16,4096]{1,0:T(8,128)(2,1)}, u32[]{:S(2)}, u32[]{:S(2)}) collective-permute-start(bf16[16,4096]{1,0:T(8,128)(2,1)S(1)} %slice.41), channel_id=1, source_target_pairs={{0,1},{1,2},{2,3},{3,4},{4,5},{5,6},{6,7},{7,8},{8,9},{9,10},{10,1... | collective-permute-start | bytes 393224 | tf_op jit(solution)/shard_map/ppermute | solution.py:20
  74.0 115.4 %collective-permute-start.1 = (bf16[16,4096]{1,0:T(8,128)(2,1)S(1)}, bf16[16,4096]{1,0:T(8,128)(2,1)}, u32[]{:S(2)}, u32[]{:S(2)}) collective-permute-start(bf16[16,4096]{1,0:T(8,128)(2,1)S(1)} %slice.43), channel_id=1, source_target_pairs={{1,0},{2,1},{3,2},{4,3},{5,4},{6,5},{7,6},{8,7},{9,8},{10,9},{11,1... | collective-permute-start | bytes 393224 | tf_op jit(solution)/shard_map/ppermute | solution.py:23
  168.1 3.9 %copy-start.12 = (s32[128,2]{0,1:T(2,128)S(1)}, s32[128,2]{0,1:T(2,128)}, u32[]{:S(2)}) copy-start(s32[128,2]{0,1:T(2,128)} %param.14) | copy-start | bytes 3076
  168.1 4.0 %copy-start.11 = (s32[128,2]{0,1:T(2,128)S(1)}, s32[128,2]{0,1:T(2,128)}, u32[]{:S(2)}) copy-start(s32[128,2]{0,1:T(2,128)} %param.13) | copy-start | bytes 3076
  168.1 4.1 %copy-start.10 = (s32[128,8]{0,1:T(8,128)S(1)}, s32[128,8]{0,1:T(8,128)}, u32[]{:S(2)}) copy-start(s32[128,8]{0,1:T(8,128)} %param.12) | copy-start | bytes 12292
  184.6 4.8 %copy-start.3 = (bf16[128,4096]{1,0:T(8,128)(2,1)S(1)}, bf16[128,4096]{1,0:T(8,128)(2,1)}, u32[]{:S(2)}) copy-start(bf16[128,4096]{1,0:T(8,128)(2,1)} %copy-done.2) | copy-start | bytes 3145732
  191.0 1.0 copy-start.5
  192.1 1.0 copy-start
  194.0 1.3 copy-start.8
  200.2 6.9 %copy-start.6 = (bf16[64,4,512]{0,1,2:T(4,128)(2,1)S(1)}, bf16[64,4,512]{0,1,2:T(4,128)(2,1)}, u32[]{:S(2)}) copy-start(bf16[64,4,512]{0,1,2:T(4,128)(2,1)} %get-tuple-element.175) | copy-start | bytes 786436 | tf_op jit(solution)/shard_map/while
  207.1 1.3 copy-start.9
  213.4 6.9 %copy-start.4 = (bf16[1024,512]{1,0:T(8,128)(2,1)S(1)}, bf16[1024,512]{1,0:T(8,128)(2,1)}, u32[]{:S(2)}) copy-start(bf16[1024,512]{1,0:T(8,128)(2,1)} %get-tuple-element.163) | copy-start | bytes 3145732 | tf_op jit(solution)/shard_map/while
  226.1 1.6 copy-start.1
  226.1 1.8 copy-start.7
  228.0 1.0 copy-start
  229.9 1.3 copy-start.8
  236.1 6.9 %copy-start.6 = (bf16[64,4,512]{0,1,2:T(4,128)(2,1)S(1)}, bf16[64,4,512]{0,1,2:T(4,128)(2,1)}, u32[]{:S(2)}) copy-start(bf16[64,4,512]{0,1,2:T(4,128)(2,1)} %get-tuple-element.175) | copy-start | bytes 786436 | tf_op jit(solution)/shard_map/while
  243.0 1.3 copy-start.9
  249.3 6.9 %copy-start.4 = (bf16[1024,512]{1,0:T(8,128)(2,1)S(1)}, bf16[1024,512]{1,0:T(8,128)(2,1)}, u32[]{:S(2)}) copy-start(bf16[1024,512]{1,0:T(8,128)(2,1)} %get-tuple-element.163) | copy-start | bytes 3145732 | tf_op jit(solution)/shard_map/while
  262.0 1.6 copy-start.1
  262.0 1.8 copy-start.7
  263.9 1.0 copy-start
  265.8 1.3 copy-start.8
  272.0 6.9 %copy-start.6 = (bf16[64,4,512]{0,1,2:T(4,128)(2,1)S(1)}, bf16[64,4,512]{0,1,2:T(4,128)(2,1)}, u32[]{:S(2)}) copy-start(bf16[64,4,512]{0,1,2:T(4,128)(2,1)} %get-tuple-element.175) | copy-start | bytes 786436 | tf_op jit(solution)/shard_map/while
  278.9 1.3 copy-start.9
  285.2 6.9 %copy-start.4 = (bf16[1024,512]{1,0:T(8,128)(2,1)S(1)}, bf16[1024,512]{1,0:T(8,128)(2,1)}, u32[]{:S(2)}) copy-start(bf16[1024,512]{1,0:T(8,128)(2,1)} %get-tuple-element.163) | copy-start | bytes 3145732 | tf_op jit(solution)/shard_map/while
  297.9 1.6 copy-start.1
  297.9 1.8 copy-start.7
  299.8 1.0 copy-start
  301.7 1.3 copy-start.8
  307.9 6.9 %copy-start.6 = (bf16[64,4,512]{0,1,2:T(4,128)(2,1)S(1)}, bf16[64,4,512]{0,1,2:T(4,128)(2,1)}, u32[]{:S(2)}) copy-start(bf16[64,4,512]{0,1,2:T(4,128)(2,1)} %get-tuple-element.175) | copy-start | bytes 786436 | tf_op jit(solution)/shard_map/while
  314.8 1.3 copy-start.9
  321.1 6.9 %copy-start.4 = (bf16[1024,512]{1,0:T(8,128)(2,1)S(1)}, bf16[1024,512]{1,0:T(8,128)(2,1)}, u32[]{:S(2)}) copy-start(bf16[1024,512]{1,0:T(8,128)(2,1)} %get-tuple-element.163) | copy-start | bytes 3145732 | tf_op jit(solution)/shard_map/while
  333.8 1.6 copy-start.1
  333.8 1.8 copy-start.7
